TPU v7x, 1024 devices: a whole 4x8x16 slice. The times are simulated.
1024 devices in a mesh: node: 64 (over x, z), local: 16 (over y, core).
Axes of the slice: x: 4, y: 8, z: 16, core: 2. Of those that a mesh axis runs over, the one named last changes fastest.
Arguments:
- tokens: bfloat16 [4096, 3584], P(('node', 'local')), may hold values from -6 to 6
- expert_ids: int32 [4096, 6], P(('node', 'local')), may hold values from 0 to 127, as said below
- gate_codes: int32 [4096, 6], P(('node', 'local')), may hold values from 1 to 1023
- gate_proj: bfloat16 [3584, 131072], P(None, ('node', 'local')), may hold values from -0.09375 to 0.09375
- up_proj: bfloat16 [3584, 131072], P(None, ('node', 'local')), may hold values from -0.09375 to 0.09375
- down_proj: bfloat16 [131072, 3584], P('node', 'local'), may hold values from -0.1875 to 0.1875
Outputs:
- routed: bfloat16 [4096, 3584], P(('node', 'local'))
Inputs may be any that keep to these rules, and one draw needn't show every extreme that they name: `expert_ids`: each token names 6 different experts, lying in exactly 4 node groups with at least one named expert in each. The tokens of one device name each node group at most 1 times in all and some node group exactly 1 times; where 64 divides 4 * 4, they name every node group exactly 1 times. For every local index, the tokens of all devices with that local index together name each node group exactly 4 * 4 times.
All inputs are finite; a program needn't handle non-finite values.
Results may differ from a plain program's by a relative error of at most 0.02.
Values may be sent and summed in bfloat16 or wider, within the bound.
A program may use at most 32 MiB of HBM per device.

v0:
```python
import jax
import jax.numpy as jnp
from jax import lax
from jax.sharding import PartitionSpec as P

FF_E = 1024
EXP_NODE = 2
NL = 4


ROUTE_SCALE = 2.5


def shortened(array):

    def short(part):
        return part.astype(jnp.bfloat16) if part.dtype == jnp.float32 else part

    return jax.tree.map(short, array)


def on_device(tokens, expert_ids, gate_codes, gate_proj, up_proj, down_proj):
    node_count = lax.axis_size("node")
    own_rows, model_width = tokens.shape
    slot_cap = -(-(own_rows * NL) // node_count)
    kept_rows = own_rows * NL
    node_of = expert_ids // EXP_NODE
    expert_side = expert_ids % EXP_NODE
    node_hit = node_of[:, :, None] == jnp.arange(node_count, dtype=jnp.int32)[None, None, :]
    code_pair = jnp.stack(
        [
            jnp.sum(
                jnp.where(
                    node_hit & (expert_side == side_index)[:, :, None], gate_codes[:, :, None], 0
                ),
                axis=1,
            )
            for side_index in range(EXP_NODE)
        ],
        axis=2,
    )
    node_used = jnp.any(node_hit, axis=1).astype(jnp.int32)
    code_total = jnp.sum(gate_codes, axis=1)
    token_info = jnp.concatenate([code_pair, (code_total[:, None] * node_used)[:, :, None]], axis=2)
    slot_rank = jnp.cumsum(node_used, axis=0) - node_used
    slot_hot = node_used[:, :, None] * (
        slot_rank[:, :, None] == jnp.arange(slot_cap, dtype=jnp.int32)[None, None, :]
    ).astype(jnp.int32)
    placing = slot_hot.astype(jnp.bfloat16)
    send_rows = jnp.einsum(
        "tnc,td->ncd", placing, tokens, preferred_element_type=jnp.float32
    ).astype(jnp.bfloat16)
    send_info = jnp.sum(slot_hot[:, :, :, None] * token_info[:, :, None, :], axis=0)
    arrived, arrived_info = (
        lax.all_to_all(send_rows, "node", split_axis=0, concat_axis=0, tiled=True),
        lax.all_to_all(send_info, "node", split_axis=0, concat_axis=0, tiled=True),
    )
    flat_rows = arrived.reshape(node_count * slot_cap, model_width)
    flat_info = arrived_info.reshape(node_count * slot_cap, EXP_NODE + 1)
    slot_live = (flat_info[:, EXP_NODE] > 0).astype(jnp.int32)
    position = jnp.cumsum(slot_live) - slot_live
    target_row = jnp.where(slot_live > 0, position, kept_rows)
    source_row = (
        jnp.zeros((kept_rows,), jnp.int32)
        .at[target_row]
        .set(jnp.arange(node_count * slot_cap, dtype=jnp.int32), mode="drop")
    )
    compact_rows = jnp.take(flat_rows, source_row, axis=0)
    compact_info = jnp.take(flat_info, source_row, axis=0)
    per_lane = gate_proj.shape[1]
    node_tokens, node_info = (
        lax.all_gather(compact_rows, "local", axis=0, tiled=True),
        lax.all_gather(shortened(compact_info), "local", axis=0, tiled=True).astype(
            compact_info.dtype
        ),
    )
    pre_gate = jnp.dot(node_tokens, gate_proj, preferred_element_type=jnp.float32)
    pre_up = jnp.dot(node_tokens, up_proj, preferred_element_type=jnp.float32)
    mine_expert = lax.axis_index("local") * per_lane // FF_E
    code_mine = jnp.sum(
        jnp.where(
            jnp.arange(EXP_NODE, dtype=jnp.int32)[None, :] == mine_expert,
            node_info[:, :EXP_NODE],
            0,
        ),
        axis=1,
    )
    gate_weight = (
        ROUTE_SCALE * code_mine.astype(jnp.float32) / node_info[:, EXP_NODE].astype(jnp.float32)
    )
    hidden = (gate_weight[:, None] * jax.nn.silu(pre_gate) * pre_up).astype(jnp.bfloat16)
    contrib = jnp.dot(
        lax.all_gather(hidden, "local", axis=1, tiled=True),
        down_proj,
        preferred_element_type=jnp.float32,
    ).astype(jnp.bfloat16)
    own_result = lax.all_to_all(contrib, "local", split_axis=0, concat_axis=1, tiled=True)
    back_index = jnp.minimum(position, kept_rows - 1)
    slot_back = jnp.where(
        slot_live[:, None] > 0,
        jnp.take(own_result, back_index, axis=0),
        jnp.zeros((), jnp.bfloat16),
    )
    returned = lax.all_to_all(
        slot_back.reshape(node_count, slot_cap, model_width),
        "node",
        split_axis=0,
        concat_axis=0,
        tiled=True,
    )
    return jnp.einsum("tnc,ncd->td", placing, returned, preferred_element_type=jnp.float32).astype(
        jnp.bfloat16
    )


def solution(mesh):
    return jax.shard_map(
        on_device,
        mesh=mesh,
        in_specs=(
            P(("node", "local"), None),
            P(("node", "local"), None),
            P(("node", "local"), None),
            P(None, ("node", "local")),
            P(None, ("node", "local")),
            P("node", "local"),
        ),
        out_specs=P(("node", "local"), None),
        check_vma=False,
    )
```

profile of v0, /device:TPU:1, one launch (start us, length us, event | category | flops | bytes accessed | tf_op | source)
XLA Modules:
  0.0 241.3 jit_solution(510833447497647572)
XLA Ops:
  6.5 0.8 add_select_fusion.1
  7.3 0.7 broadcast_compare_fusion.3
  8.0 0.1 copy.25
  8.1 0.1 fusion.10
  8.2 0.8 copy.27
  9.0 0.8 reduce_sum.49
  9.8 0.1 copy.26
  9.9 0.1 copy.28
  10.1 0.1 select_reduce_fusion.1
  10.2 0.7 copy.29
  10.9 22.8 %all-to-all-start = ((s32[64,1,3]{2,1,0:T(1,128)}), s32[64,1,3]{2,1,0:T(1,128)S(1)}, u32[]{:S(2)}, u32[]{:S(2)}) async-start(s32[64,1,3]{2,1,0:T(1,128)} %copy.29), calls=%async_computation | async-start | bytes 65536 | tf_op jit(solution)/shard_map/all_to_all | solution.py:56
  33.7 1.1 fusion
  34.8 0.5 broadcast.272
  35.3 0.9 reduce.9
  36.2 0.9 reshape.261
  37.1 9.8 %all-to-all-done = s32[64,1,3]{2,1,0:T(1,128)S(1)} async-done(((s32[64,1,3]{2,1,0:T(1,128)}), s32[64,1,3]{2,1,0:T(1,128)S(1)}, u32[]{:S(2)}, u32[]{:S(2)}) %all-to-all-start) | async-done | bytes 800 | tf_op jit(solution)/shard_map/all_to_all | solution.py:56
  46.8 4.8 %all-to-all-start.1 = ((bf16[64,2,1792]{2,1,0:T(2,128)(2,1)}), bf16[64,2,1792]{2,1,0:T(2,128)(2,1)S(1)}, u32[]{:S(2)}, u32[]{:S(2)}) async-start(bf16[64,2,1792]{2,1,0:T(2,128)(2,1)} %reshape.261), calls=%async_computation.1 | async-start | bytes 917504 | tf_op jit(solution)/shard_map/all_to_all | solution.py:55
  51.7 0.1 fusion.6
  51.8 0.1 reduce-window.4
  51.9 0.2 fusion.20
  52.1 0.2 fusion.7
  52.3 0.8 scatter_custom_fusion
  53.1 24.2 %all-to-all-done.1 = bf16[64,2,1792]{2,1,0:T(2,128)(2,1)S(1)} async-done(((bf16[64,2,1792]{2,1,0:T(2,128)(2,1)}), bf16[64,2,1792]{2,1,0:T(2,128)(2,1)S(1)}, u32[]{:S(2)}, u32[]{:S(2)}) %all-to-all-start.1) | async-done | bytes 458784 | tf_op jit(solution)/shard_map/all_to_all | solution.py:55
  77.3 0.4 reshape.262
  77.8 0.6 gather_fusion.1
  78.4 0.7 broadcast_select_fusion
  79.2 0.6 gather_fusion
  79.8 0.1 broadcast_select_fusion.1
  79.8 0.1 copy.30
  79.9 21.6 %all-gather = s32[16,16,3]{1,2,0:T(4,128)S(1)} all-gather(s32[1,16,3]{1,2,0:T(4,128)S(1)} %bitcast.43), channel_id=1, replica_groups=mesh['node'=64,'local'=16] {'local'}, dimensions={0}, use_global_device_ids=true | all-gather | bytes 3264 | tf_op jit(solution)/shard_map/all_gather | solution.py:73
  101.5 0.1 reshape.254
  101.6 0.1 fusion.12
  101.7 20.8 %all-gather.4.cloned.1.call-done = bf16[256,3584]{1,0:T(8,128)(2,1)} async-done(((bf16[16,3584]{1,0:T(8,128)(2,1)}), bf16[256,3584]{1,0:T(8,128)(2,1)}) %all-gather.4.cloned.1.call-update) | async-done | bytes 1835024 | tf_op jit(solution)/shard_map/all_gather | solution.py:72
  122.5 2.3 fusion.21
  124.8 1.3 fusion.1
  126.1 44.5 %all-gather.6.cloned.1.call-done = bf16[256,2048]{1,0:T(8,128)(2,1)} async-done(((bf16[256,128]{1,0:T(8,128)(2,1)}), bf16[256,2048]{1,0:T(8,128)(2,1)}) %all-gather.6.cloned.1.call-update) | async-done | bytes 1048592 | tf_op jit(solution)/shard_map/all_gather | solution.py:93
  170.6 1.7 convolution_convert_fusion.2
  172.3 0.7 copy.33
  173.0 5.4 %all-to-all-start.2 = ((bf16[16,16,224]{2,1,0:T(8,128)(2,1)}), bf16[16,16,224]{2,1,0:T(8,128)(2,1)S(1)}, u32[]{:S(2)}, u32[]{:S(2)}) async-start(bf16[16,16,224]{2,1,0:T(8,128)(2,1)} %bitcast.10), calls=%async_computation.2 | async-start | bytes 262144 | tf_op jit(solution)/shard_map/all_to_all | solution.py:97
  178.4 8.9 %all-to-all-done.2 = bf16[16,16,224]{2,1,0:T(8,128)(2,1)S(1)} async-done(((bf16[16,16,224]{2,1,0:T(8,128)(2,1)}), bf16[16,16,224]{2,1,0:T(8,128)(2,1)S(1)}, u32[]{:S(2)}, u32[]{:S(2)}) %all-to-all-start.2) | async-done | bytes 114720 | tf_op jit(solution)/shard_map/all_to_all | solution.py:97
  187.3 0.2 all_to_all.28
  187.5 0.8 gather_fusion.2
  188.4 0.1 fusion.4
  188.5 0.9 reduce.10
  189.4 0.1 reshape.263
  189.5 43.8 %all_to_all.34 = bf16[64,2,1792]{2,1,0:T(2,128)(2,1)S(1)} all-to-all(bf16[64,2,1792]{2,1,0:T(2,128)(2,1)S(1)} %reshape.263), channel_id=1, replica_groups=mesh['node'=64,'local'=16] {'node'}, dimensions={0} | all-to-all | bytes 917504 | tf_op jit(solution)/shard_map/all_to_all | solution.py:104
  233.3 0.4 reshape.264
  233.7 0.8 convolution_convert_fusion.1
  (28 shorter events, 0.4 us)
Async XLA Ops:
  6.5 164.0 %copy-start = (bf16[2048,224]{0,1:T(8,128)(2,1)S(1)}, bf16[2048,224]{0,1:T(8,128)(2,1)}, u32[]{:S(2)}) copy-start(bf16[2048,224]{0,1:T(8,128)(2,1)} %param.11) | copy-start | bytes 2752516
  10.9 35.9 %all-to-all-start = ((s32[64,1,3]{2,1,0:T(1,128)}), s32[64,1,3]{2,1,0:T(1,128)S(1)}, u32[]{:S(2)}, u32[]{:S(2)}) async-start(s32[64,1,3]{2,1,0:T(1,128)} %copy.29), calls=%async_computation | async-start | bytes 65536 | tf_op jit(solution)/shard_map/all_to_all | solution.py:56
  46.8 30.5 %all-to-all-start.1 = ((bf16[64,2,1792]{2,1,0:T(2,128)(2,1)}), bf16[64,2,1792]{2,1,0:T(2,128)(2,1)S(1)}, u32[]{:S(2)}, u32[]{:S(2)}) async-start(bf16[64,2,1792]{2,1,0:T(2,128)(2,1)} %reshape.261), calls=%async_computation.1 | async-start | bytes 917504 | tf_op jit(solution)/shard_map/all_to_all | solution.py:55
  51.7 70.8 %all-gather.4.cloned.1.call-start = ((), (), s32[]{:S(2)}) async-start(), calls=%async_computation.4 | async-start | bytes 1949696 | tf_op jit(solution)/shard_map/all_gather | solution.py:72
  77.7 44.8 %copy-start.2 = (bf16[3584,128]{1,0:T(8,128)(2,1)S(1)}, bf16[3584,128]{1,0:T(8,128)(2,1)}, u32[]{:S(2)}) copy-start(bf16[3584,128]{1,0:T(8,128)(2,1)} %param.9) | copy-start | bytes 2752516
  79.1 45.6 %copy-start.3 = (bf16[3584,128]{1,0:T(8,128)(2,1)S(1)}, bf16[3584,128]{1,0:T(8,128)(2,1)}, u32[]{:S(2)}) copy-start(bf16[3584,128]{1,0:T(8,128)(2,1)} %param.10) | copy-start | bytes 2752516
  79.1 91.4 %all-gather.6.cloned.1.call-start = ((), (), s32[]{:S(2)}) async-start(), calls=%async_computation.5 | async-start | bytes 1114112 | tf_op jit(solution)/shard_map/all_gather | solution.py:93
  122.5 2.3 copy-start.1
  173.0 14.3 %all-to-all-start.2 = ((bf16[16,16,224]{2,1,0:T(8,128)(2,1)}), bf16[16,16,224]{2,1,0:T(8,128)(2,1)S(1)}, u32[]{:S(2)}, u32[]{:S(2)}) async-start(bf16[16,16,224]{2,1,0:T(8,128)(2,1)} %bitcast.10), calls=%async_computation.2 | async-start | bytes 262144 | tf_op jit(solution)/shard_map/all_to_all | solution.py:97
Sparse Core Ops, SparseCore 0:
  79.2 43.1 all-gather.3
  126.2 44.3 all-gather.5
where the time goes:
time: 243 us; the launch traced here: 241 us
  waiting for transfers between devices  108 us (44%)
  blocking collectives  65.4 us (27%)
  starting transfers between devices  33 us (14%)
  between operations  13.6 us (6%)
  local copies, waits for them, and re-layouts  7.98 us (3%)
  matrix products  7.1 us (3%)
  other arithmetic  6.04 us (2%)
    all_gather x1, waiting for transfers between devices, on_device(): lax.all_gather(hidden, 'local', axis=1, tiled=True)  44.5 us
    all_to_all x1, blocking collectives, on_device(): lax.all_to_all(slot_back.reshape(node_count, slot_cap, model_width), 'nod...  43.8 us
    all_to_all x1, waiting for transfers between devices, on_device(): lax.all_to_all(send_rows, 'node', split_axis=0, concat_axis=0, tiled=True)  24.2 us
    all_to_all x1, starting transfers between devices, on_device(): lax.all_to_all(send_info, 'node', split_axis=0, concat_axis=0, tiled=True)  22.8 us
    all_gather x1, blocking collectives, on_device(): lax.all_gather(shortened(compact_info), 'local', axis=0, tiled=True)  21.6 us
    all_gather x1, waiting for transfers between devices, on_device(): lax.all_gather(compact_rows, 'local', axis=0, tiled=True)  20.8 us
    all_to_all x1, waiting for transfers between devices, on_device(): lax.all_to_all(send_info, 'node', split_axis=0, concat_axis=0, tiled=True)  9.76 us
    all_to_all x1, waiting for transfers between devices, on_device(): lax.all_to_all(contrib, 'local', split_axis=0, concat_axis=1, tiled=True)  8.88 us
  transfers between devices with their start and end apart: 5, of which 5 were waited for; matrix products, arithmetic and copies ran while one was open for 2% of the time, Pallas kernels for 0%

commit v1 on v0

v1 whole, which is shorter than its diff:
```python
import functools

import jax
import jax.numpy as jnp
from jax import lax
from jax.experimental import pallas as pl
from jax.experimental.pallas import tpu as pltpu
from jax.sharding import PartitionSpec as P

NX, NZ, NY = 4, 16, 8
TOK = 4
SEG = 4
ROWS = 16
FF_E = 1024
ROUTE_SCALE = 2.5
SENDS = 64
MESH = pl.DeviceIdType.MESH
F32, BF16, I32 = jnp.float32, jnp.bfloat16, jnp.int32


def log2(n):
    return n.bit_length() - 1


def dot(a, b):
    return jnp.dot(a, b, preferred_element_type=F32)


def dot_nt(a, b):
    return lax.dot_general(a, b, (((1,), (1,)), ((), ())), preferred_element_type=F32)


def iota(shape, axis):
    return lax.broadcasted_iota(I32, shape, axis)


def hot(mask):
    return jnp.where(mask, 1.0, 0.0).astype(BF16)


def arrival_order():
    order = [0]
    for k in range(1, NZ // 2):
        order += [k, NZ - k]
    return order + [NZ // 2]


class Sender:
    def __init__(self, sems):
        self.sems, self.live, self.count = sems, {}, 0

    def __call__(self, src, dst, recv_sem, device):
        slot = self.count % SENDS
        if slot in self.live:
            self.live[slot].wait_send()
        copy = pltpu.make_async_remote_copy(
            src_ref=src, dst_ref=dst, send_sem=self.sems.at[slot], recv_sem=recv_sem,
            device_id=device, device_id_type=MESH,
        )
        copy.start()
        self.live[slot] = copy
        self.count += 1

    def arrived(self, dst, recv_sem, device):
        pltpu.make_async_remote_copy(
            src_ref=dst, dst_ref=dst, send_sem=self.sems.at[0], recv_sem=recv_sem,
            device_id=device, device_id_type=MESH,
        ).wait_recv()

    def drain(self):
        for copy in self.live.values():
            copy.wait_send()


def kernel(tok_ref, ids_ref, codes_ref, gate_hbm, up_hbm, down_hbm, out_ref,
           w_in, w_down, zb, xs, xr, xg, xm, hg, acc, ex, rs, rr, sb, rb, fs, fr,
           wsem, ssem, zsem, xsem, ysem, ymsem, psem, pmsem, hsem, hpsem, rsem, bsem, fsem):
    lanes_n = 2 * NY
    width = tok_ref.shape[1]
    seg_len = width // SEG
    feats = down_hbm.shape[0]
    half = NY // 2

    node, loc = lax.axis_index("node"), lax.axis_index("local")
    x, z = lax.div(node, NZ), lax.rem(node, NZ)
    y, core = lax.div(loc, 2), lax.rem(loc, 2)
    z_right = (x * NZ + lax.rem(z + 1, NZ), loc)
    z_left = (x * NZ + lax.rem(z + NZ - 1, NZ), loc)

    def x_dev(d):
        return (lax.rem(x + d, NX) * NZ + z, loc)

    def chip(d):
        return lax.rem(y + d + NY, NY)

    y_devs = ((node, chip(1) * 2 + core), (node, chip(-1) * 2 + core))
    partner = (node, y * 2 + 1 - core)

    barrier = pltpu.get_barrier_semaphore()
    friends = [z_right, z_left] + [x_dev(d) for d in range(1, NX)]
    friends += [(node, lax.rem(loc + k, lanes_n)) for k in range(1, lanes_n)]
    for friend in friends:
        pl.semaphore_signal(barrier, inc=1, device_id=friend, device_id_type=MESH)

    weight_copies = [
        pltpu.make_async_copy(gate_hbm, w_in.at[:, pl.ds(0, 128)], wsem.at[0]),
        pltpu.make_async_copy(up_hbm, w_in.at[:, pl.ds(128, 128)], wsem.at[1]),
        pltpu.make_async_copy(down_hbm, w_down.at[pl.ds(0, feats)], wsem.at[2]),
    ]
    for copy in weight_copies:
        copy.start()
    if feats < 256:
        w_down[pl.ds(feats, 256 - feats), :] = jnp.zeros((256 - feats, w_down.shape[1]), BF16)

    tokens = tok_ref[...].astype(F32)
    lane4 = iota((TOK, 128), 1)
    ids, codes = ids_ref[...], codes_ref[...].astype(F32)
    total = jnp.sum(codes, axis=1, keepdims=True)
    dense = jnp.zeros((TOK, 128), F32)
    for p in range(ids.shape[1]):
        dense += jnp.where(lane4 == ids[:, p : p + 1], codes[:, p : p + 1], 0.0)
    dense = ROUTE_SCALE * dense / total
    zb[0, :, pl.ds(0, seg_len)] = jnp.concatenate(
        [tokens[:, s * seg_len : (s + 1) * seg_len] for s in range(SEG)], axis=0
    ).astype(BF16)
    zb[0, :, pl.ds(seg_len, 128)] = jnp.concatenate([dense] * SEG, axis=0).astype(BF16)

    pl.semaphore_wait(barrier, len(friends))
    send = Sender(ssem)

    order = arrival_order()
    at = {j: p for p, j in enumerate(order)}
    sel_rows = NX * 16
    row = iota((sel_rows, 64), 0)
    col = iota((sel_rows, 64), 1)
    same_seg_block = (((row >> 2) & 3) == ((col >> 2) & 3)) & ((row & 3) == (col >> 4))
    row_e = iota((sel_rows, 128), 0)
    lane_e = iota((sel_rows, 128), 1)
    goal = ((x + (row_e >> 4)) & (NX - 1)) * NZ + z
    goal_hot = hot((lane_e >> 1) == goal)
    token_lane = lane_e == ((2 * goal + 2) & 127)
    token_value = ((iota((64, 128), 0) & 3) + 1).astype(F32).astype(BF16)

    def select(q):
        block = zb[pl.ds(4 * q, 4)].reshape(64, seg_len + 128)
        body, meta = block[:, :seg_len], block[:, seg_len:]
        picks = hot((dot_nt(goal_hot, meta) > 0.0) & same_seg_block)
        rows = dot(picks, body).astype(BF16)
        info = jnp.where(token_lane, dot(picks, token_value), dot(picks, meta)).astype(BF16)
        for d in list(range(1, NX)) + [0]:
            target = xs if d else xr
            target[d, q, :, pl.ds(0, seg_len)] = rows[d * 16 : (d + 1) * 16]
            target[d, q, :, pl.ds(seg_len, 128)] = info[d * 16 : (d + 1) * 16]
            if d:
                send(xs.at[d, q], xr.at[d, q], xsem.at[d, q], x_dev(d))

    def z_hop(j, j_there, device):
        send(zb.at[at[j]], zb.at[at[j_there]], zsem.at[at[j_there]], device)

    z_hop(0, 1, z_right)
    z_hop(0, NZ - 1, z_left)
    here, done = {0}, 0
    for k in range(1, NZ // 2 + 1):
        send.arrived(zb.at[at[k]], zsem.at[at[k]], z_left)
        here.add(at[k])
        if k < NZ // 2:
            z_hop(k, k + 1, z_right)
        if k < NZ // 2:
            j = NZ - k
            send.arrived(zb.at[at[j]], zsem.at[at[j]], z_right)
            here.add(at[j])
            if j - 1 > NZ // 2:
                z_hop(j, j - 1, z_left)
        while done < NZ // 4 and all(p in here for p in range(4 * done, 4 * done + 4)):
            select(done)
            done += 1

    for q in range(NZ // 4):
        for d in range(1, NX):
            send.arrived(xr.at[d, q], xsem.at[d, q], x_dev(NX - d))

    slots = NX * NZ * SEG
    gate_lane = 2 * node
    token_at = (2 * node + 2) & 127
    source_at = (2 * node + 3) & 127
    every = xr[...].reshape(slots, seg_len + 128)
    meta = every[:, seg_len:]
    live = dot_nt(hot(iota((SEG * ROWS, 128), 1) == token_at), meta) > 0.0
    ahead_r, ahead_c = iota((slots, slots), 0), iota((slots, slots), 1)

    def slot_of(r):
        return (r >> 4) * 4 + (r & 3)

    ahead = hot((((ahead_r >> 2) & 3) == ((ahead_c >> 2) & 3)) & (slot_of(ahead_r) < slot_of(ahead_c)))
    place = dot(hot(live), ahead)
    want_r, want_c = iota((SEG * ROWS, slots), 0), iota((SEG * ROWS, slots), 1)
    picks = hot(
        live & (place == (want_r & (ROWS - 1)).astype(F32)) & ((want_r >> 4) == ((want_c >> 2) & 3))
    )
    xg[loc] = dot(picks, every[:, :seg_len]).astype(BF16).reshape(SEG, ROWS, seg_len)
    slot_value = slot_of(iota((slots, 128), 0)).astype(F32).astype(BF16)
    first = picks[:ROWS]
    xm[loc] = jnp.where(
        iota((ROWS, 128), 1) == source_at, dot(first, slot_value), dot(first, meta)
    ).astype(BF16)

    def chip_lane(d, other=False):
        return chip(d) * 2 + (1 - core if other else core)

    def y_part(lane, h):
        return xg.at[lane, pl.ds(2 * h, 2)]

    def y_hop(way, k, lane, h):
        send(y_part(lane, h), y_part(lane, h), ysem.at[way, k, h], y_devs[way])
        if h == way and not (k == half and way):
            send(xm.at[lane], xm.at[lane], ymsem.at[way, k], y_devs[way])

    def y_wait(way, k, lane, h):
        send.arrived(y_part(lane, h), ysem.at[way, k, h], y_devs[1 - way])
        if h == way and not (k == half and way):
            send.arrived(xm.at[lane], ymsem.at[way, k], y_devs[1 - way])

    def p_hop(d, lane, h, with_meta):
        send(y_part(lane, h), y_part(lane, h), psem.at[d % NY, h], partner)
        if with_meta:
            send(xm.at[lane], xm.at[lane], pmsem.at[d % NY], partner)

    def p_wait(d):
        lane = chip_lane(d, True)
        for h in range(2):
            send.arrived(y_part(lane, h), psem.at[d % NY, h], partner)
        send.arrived(xm.at[lane], pmsem.at[d % NY], partner)

    def passes(k, way, h):
        return k < half or (k == half and h == way)

    my_expert = lax.div(loc * 128, FF_E)

    def gate_up(chips):
        lanes = []
        for d in chips:
            p_wait(d)
            lanes += [chip_lane(d), chip_lane(d, True)]
        lhs = jnp.concatenate(
            [jnp.concatenate([xg[lane, s] for lane in lanes], axis=0) for s in range(SEG)], axis=1
        )
        pre = dot(lhs, w_in[...])
        info = jnp.concatenate([xm[lane] for lane in lanes], axis=0).astype(F32)
        gate = jnp.sum(
            jnp.where(iota(info.shape, 1) == gate_lane + my_expert, info, 0.0), axis=1, keepdims=True
        )
        g, u = pre[:, :128], pre[:, 128:]
        hidden = (gate * (g / (1.0 + jnp.exp(-g))) * u).astype(BF16)
        for n, lane in enumerate(lanes):
            hg[loc, lane] = hidden[n * ROWS : (n + 1) * ROWS]

    for h in range(2):
        for way in range(2):
            if passes(1, way, h):
                y_hop(way, 1, loc, h)
        p_hop(0, loc, h, h == 0)
    for copy in weight_copies:
        copy.wait()
    for k in range(1, half + 1):
        for h in range(2):
            for way in range(2):
                if passes(k, way, h):
                    d = -k if way == 0 else k
                    lane = chip_lane(d)
                    y_wait(way, k, lane, h)
                    if passes(k + 1, way, h):
                        y_hop(way, k + 1, lane, h)
                    p_hop(d, lane, h, h == way if k < half else way == 0)
        gate_up([0] if k == 1 else [-(k - 1), k - 1])
    gate_up([half])

    def h_part(lane, h):
        return hg.at[lane, pl.ds(h * NY, NY)]

    def h_hop(way, k, lane, h):
        send(h_part(lane, h), h_part(lane, h), hsem.at[way, k, h], y_devs[way])

    def hp_hop(d, lane, h):
        send(h_part(lane, h), h_part(lane, h), hpsem.at[d % NY, h], partner)

    for h in range(2):
        for way in range(2):
            if passes(1, way, h):
                h_hop(way, 1, loc, h)
        hp_hop(0, loc, h)

    group_rows = lanes_n * ROWS
    back_rows = NZ * lanes_n
    info = xm[...].reshape(group_rows, 128)
    source = dot_nt(hot(iota((back_rows, 128), 1) == source_at), info)
    back_r, back_c = iota((back_rows, group_rows), 0), iota((back_rows, group_rows), 1)
    lane_match = (back_r & (lanes_n - 1)) == (back_c >> 4)
    back_slot = NZ - 1 - (back_r >> log2(lanes_n))
    for d in range(NX):
        ex[d] = hot(lane_match & (source == (back_slot + d * NZ).astype(F32)))
    token_col = jnp.sum(
        jnp.where(iota((group_rows, 128), 1) == token_at, info.astype(F32), 0.0), axis=1, keepdims=True
    )

    acc[...] = jnp.zeros(acc.shape, F32)

    def down(chips):
        for d in chips:
            for h in range(2):
                send.arrived(h_part(chip_lane(d, True), h), hpsem.at[d % NY, h], partner)
            lhs = jnp.concatenate(
                [hg[chip(d) * 2 + c].reshape(group_rows, 128) for c in range(2)], axis=1
            )
            at_col = pl.multiple_of(chip(d) * 256, 256)
            acc[...] += dot_nt(lhs, w_down[:, pl.ds(at_col, 256)])

    for k in range(1, half + 1):
        for h in range(2):
            for way in range(2):
                if passes(k, way, h):
                    d = -k if way == 0 else k
                    lane = chip_lane(d)
                    send.arrived(h_part(lane, h), hsem.at[way, k, h], y_devs[1 - way])
                    if passes(k + 1, way, h):
                        h_hop(way, k + 1, lane, h)
                    hp_hop(d, lane, h)
        down([0] if k == 1 else [-(k - 1), k - 1])
    down([half])

    result = jnp.where(iota((group_rows, 256), 1) == feats, token_col, acc[...]).astype(BF16)
    for q in range(NZ // 4):
        for d in list(range(1, NX)) + [0]:
            rows = dot(ex[d, pl.ds(q * 4 * lanes_n, 4 * lanes_n)], result).astype(BF16)
            target = rs if d else rr
            target[d, pl.ds(4 * q, 4)] = rows.reshape(4, lanes_n, 256)
            if d:
                send(rs.at[d, pl.ds(4 * q, 4)], rr.at[d, pl.ds(4 * q, 4)], rsem.at[d, q], x_dev(NX - d))

    seen = set()

    def part(j):
        p = NZ - 1 - at[j]
        q = p // 4
        if q not in seen:
            seen.add(q)
            for d in range(1, NX):
                send.arrived(rr.at[d, pl.ds(4 * q, 4)], rsem.at[d, q], x_dev(d))
        sums = [jnp.zeros((lanes_n, 256), F32) for t in range(TOK)]
        for d in range(NX):
            rows = rr[d, p].astype(F32)
            which = jnp.sum(
                jnp.where(iota((lanes_n, 256), 1) == feats, rows, 0.0), axis=1, keepdims=True
            )
            for t in range(TOK):
                sums[t] += jnp.where(which == float(t + 1), rows, 0.0)
        return jnp.concatenate(sums, axis=0)

    for s in range(NZ // 2):
        for j, step, device, source_dev in (
            (NZ // 2 - s, -1, z_left, z_right),
            (NZ // 2 + 1 + s, 1, z_right, z_left),
        ):
            if j >= NZ:
                continue
            value = part(j)
            if s:
                send.arrived(rb.at[j], bsem.at[j], source_dev)
                value += rb[j].astype(F32)
            sb[j] = value.astype(BF16)
            send(sb.at[j], rb.at[j + step], bsem.at[j + step], device)
    value = part(0)
    send.arrived(rb.at[NZ], bsem.at[NZ], z_left)
    value += rb[NZ].astype(F32)
    send.arrived(rb.at[0], bsem.at[0], z_right)
    value = (value + rb[0].astype(F32)).astype(BF16)

    fin_r, fin_c = iota((lanes_n * 8, TOK * lanes_n), 0), iota((lanes_n * 8, TOK * lanes_n), 1)
    fin = ((fin_r >> 3) == (fin_c & (lanes_n - 1))) & ((fin_r & 3) == (fin_c >> log2(lanes_n)))
    upper = ((fin_r >> 2) & 1) == 1
    rows = dot(hot(fin & jnp.logical_not(upper)), value[:, :128]) + dot(hot(fin & upper), value[:, 128:])
    fs[...] = rows.astype(BF16).reshape(lanes_n, 8, 128)
    for k in range(1, lanes_n):
        lane = lax.rem(loc + k, lanes_n)
        send(fs.at[lane], fr.at[loc], fsem.at[k], (node, lane))
    out_ref[loc] = fs[loc]
    for k in range(1, lanes_n):
        lane = lax.rem(loc + lanes_n - k, lanes_n)
        send.arrived(fr.at[lane], fsem.at[k], (node, lane))
        out_ref[lane] = fr[lane]
    send.drain()


def on_device(tokens, expert_ids, gate_codes, gate_proj, up_proj, down_proj):
    width = tokens.shape[1]
    seg_len = width // SEG
    lanes_n = 2 * NY
    hidden, feats = down_proj.shape
    dma = pltpu.SemaphoreType.DMA
    vmem = pl.BlockSpec(memory_space=pltpu.VMEM)
    hbm = pl.BlockSpec(memory_space=pltpu.HBM)
    half = NY // 2
    pieces = pl.pallas_call(
        kernel,
        out_shape=jax.ShapeDtypeStruct((lanes_n, 8, 128), BF16),
        in_specs=[vmem, vmem, vmem, hbm, hbm, hbm],
        out_specs=vmem,
        scratch_shapes=[
            pltpu.VMEM((width, 256), BF16),
            pltpu.VMEM((256, hidden), BF16),
            pltpu.VMEM((NZ, 16, seg_len + 128), BF16),
            pltpu.VMEM((NX, NZ // 4, 16, seg_len + 128), BF16),
            pltpu.VMEM((NX, NZ // 4, 16, seg_len + 128), BF16),
            pltpu.VMEM((lanes_n, SEG, ROWS, seg_len), BF16),
            pltpu.VMEM((lanes_n, ROWS, 128), BF16),
            pltpu.VMEM((lanes_n, lanes_n, ROWS, 128), BF16),
            pltpu.VMEM((lanes_n * ROWS, 256), F32),
            pltpu.VMEM((NX, NZ * lanes_n, lanes_n * ROWS), BF16),
            pltpu.VMEM((NX, NZ, lanes_n, 256), BF16),
            pltpu.VMEM((NX, NZ, lanes_n, 256), BF16),
            pltpu.VMEM((NZ, TOK * lanes_n, 256), BF16),
            pltpu.VMEM((NZ + 1, TOK * lanes_n, 256), BF16),
            pltpu.VMEM((lanes_n, 8, 128), BF16),
            pltpu.VMEM((lanes_n, 8, 128), BF16),
            dma((3,)),
            dma((SENDS,)),
            dma((NZ,)),
            dma((NX, NZ // 4)),
            dma((2, half + 1, 2)),
            dma((2, half + 1)),
            dma((NY, 2)),
            dma((NY,)),
            dma((2, half + 1, 2)),
            dma((NY, 2)),
            dma((NX, NZ // 4)),
            dma((NZ + 1,)),
            dma((lanes_n,)),
        ],
        compiler_params=pltpu.CompilerParams(
            collective_id=0, has_side_effects=True, vmem_limit_bytes=48 << 20
        ),
        name="moe",
    )(tokens, expert_ids, gate_codes, gate_proj, up_proj, down_proj.T)
    pieces = pieces.reshape(lanes_n, 2, TOK, 128).transpose(2, 0, 1, 3).reshape(TOK, lanes_n, 256)
    return pieces[:, :, :feats].reshape(TOK, width)


def solution(mesh):
    return jax.shard_map(
        on_device,
        mesh=mesh,
        in_specs=(
            P(("node", "local"), None),
            P(("node", "local"), None),
            P(("node", "local"), None),
            P(None, ("node", "local")),
            P(None, ("node", "local")),
            P("node", "local"),
        ),
        out_specs=P(("node", "local"), None),
        check_vma=False,
    )
```

time: 243 us -> 124 us (0.51)
  Pallas kernels: 0 us -> 117 us
  waiting for transfers between devices: 108 us -> 0 us
  blocking collectives: 65.4 us -> 0 us
  starting transfers between devices: 33 us -> 0 us
  between operations: 13.6 us -> 0.03 us
  matrix products: 7.1 us -> 0 us
  other arithmetic: 6.04 us -> 0 us
    pallas_call x0 -> x1, Pallas kernels: none -> 117 us  [on_device(): pl.pallas_call(kernel, out_shape=jax.ShapeDtypeStruct((lanes_n, 8, 128),...]
    all_gather x2 -> x0, waiting for transfers between devices: 65.3 us -> none  [the longest x1 44.5 us: on_device(): lax.all_gather(hidden, 'local', axis=1, tiled=True)]
    all_to_all x1 -> x0, blocking collectives: 43.8 us -> none  [on_device(): lax.all_to_all(slot_back.reshape(node_count, slot_cap, model_width), 'nod...]
    all_to_all x3 -> x0, waiting for transfers between devices: 42.8 us -> none  [the longest x1 24.2 us: on_device(): lax.all_to_all(send_rows, 'node', split_axis=0, concat_axis=0, tiled=True)]
    all_to_all x3 -> x0, starting transfers between devices: 32.9 us -> none  [the longest x1 22.8 us: on_device(): lax.all_to_all(send_info, 'node', split_axis=0, concat_axis=0, tiled=True)]
    all_gather x1 -> x0, blocking collectives: 21.6 us -> none  [on_device(): lax.all_gather(shortened(compact_info), 'local', axis=0, tiled=True)]
    dot_general x5 -> x0, matrix products: 7.1 us -> none  [the longest x1 2.26 us: on_device(): jnp.dot(node_tokens, gate_proj, preferred_element_type=jnp.float32)]
    unnamed x15 -> x12, local copies, waits for them, and re-layouts: 2.63 us -> 5.64 us
  transfers between devices with their start and end apart: 5 -> 0, of which waited for: 5 -> 0; matrix products, arithmetic and copies ran while one was open for 2% -> 0% of each run, Pallas kernels for 0% -> 0%
where the time goes in v1:
time: 124 us
  Pallas kernels  117 us (94%)
  local copies, waits for them, and re-layouts  6.42 us (5%)
    pallas_call x1, Pallas kernels, on_device(): pl.pallas_call(kernel, out_shape=jax.ShapeDtypeStruct((lanes_n, 8, 128),...  117 us
    unnamed x12, local copies, waits for them, and re-layouts  5.64 us

profile of v1, /device:TPU:1, one launch (start us, length us, event | category | flops | bytes accessed | tf_op | source)
XLA Modules:
  0.0 123.9 jit_solution(16413333885583332843)
XLA Ops:
  0.0 0.0 copy-start
  0.0 1.2 copy-done
  1.2 0.0 copy-start.1
  1.2 1.2 copy-done.1
  2.4 0.0 copy-start.2
  2.4 1.2 copy-done.2
  3.5 0.0 copy-start.3
  3.5 0.7 copy-done.3
  4.3 0.0 copy-start.4
  4.3 0.7 copy-done.4
  5.0 0.0 copy-start.5
  5.0 0.7 copy-done.5
  5.7 117.4 %moe.1 = bf16[16,8,128]{2,1,0:T(8,128)(2,1)S(1)} custom-call(bf16[4,3584]{1,0:T(4,128)(2,1)S(1)} %copy-done.3, s32[4,6]{1,0:T(4,128)S(1)} %copy-done.4, s32[4,6]{1,0:T(4,128)S(1)} %copy-done.5, bf16[3584,128]{1,0:T(8,128)(2,1)S(1)} %copy-done, bf16[3584,128]{1,0:T(8,128)(2,1)S(1)} %copy-done.1, bf16[224,2048]{1,0:T(8,128)(2,1)S(1)} %bitcast.6), custom_call_target="tpu_custom_call" | custom-call | tf_op jit(solution)/shard_map/moe/pallas_call | solution.py:402
  123.2 0.7 reshape.11
  (2 shorter events, 0.1 us)
Async XLA Ops:
  0.0 1.2 copy-start
  1.2 1.2 copy-start.1
  2.4 1.2 copy-start.2
  3.5 0.7 copy-start.3
  4.3 0.7 copy-start.4
  5.0 0.7 copy-start.5

commit v2 on v1

--- a/solution.py
+++ b/solution.py
@@ -14,6 +14,8 @@
 FF_E = 1024
 ROUTE_SCALE = 2.5
 SENDS = 64
+STRIDE = 2
+PARTS = 2
 MESH = pl.DeviceIdType.MESH
 F32, BF16, I32 = jnp.float32, jnp.bfloat16, jnp.int32
 
@@ -72,11 +74,11 @@
             copy.wait_send()
 
 
-def kernel(tok_ref, ids_ref, codes_ref, gate_hbm, up_hbm, down_hbm, out_ref,
-           w_in, w_down, zb, xs, xr, xg, xm, hg, acc, ex, rs, rr, sb, rb, fs, fr,
+def kernel(tok_hbm, ids_hbm, codes_hbm, gate_hbm, up_hbm, down_hbm, out_ref,
+           tok_ref, ids_ref, codes_ref, w_in, w_down, zb, xs, xr, xg, xm, hg, acc, token_col, ex, rs, rr, sb, rb, fs, fr,
            wsem, ssem, zsem, xsem, ysem, ymsem, psem, pmsem, hsem, hpsem, rsem, bsem, fsem):
     lanes_n = 2 * NY
-    width = tok_ref.shape[1]
+    width = tok_hbm.shape[1]
     seg_len = width // SEG
     feats = down_hbm.shape[0]
     half = NY // 2
@@ -84,8 +86,9 @@
     node, loc = lax.axis_index("node"), lax.axis_index("local")
     x, z = lax.div(node, NZ), lax.rem(node, NZ)
     y, core = lax.div(loc, 2), lax.rem(loc, 2)
-    z_right = (x * NZ + lax.rem(z + 1, NZ), loc)
-    z_left = (x * NZ + lax.rem(z + NZ - 1, NZ), loc)
+
+    def z_dev(d):
+        return (x * NZ + lax.rem(z + d + NZ, NZ), loc)
 
     def x_dev(d):
         return (lax.rem(x + d, NX) * NZ + z, loc)
@@ -96,8 +99,16 @@
     y_devs = ((node, chip(1) * 2 + core), (node, chip(-1) * 2 + core))
     partner = (node, y * 2 + 1 - core)
 
+    input_copies = [
+        pltpu.make_async_copy(tok_hbm, tok_ref, wsem.at[3]),
+        pltpu.make_async_copy(ids_hbm, ids_ref, wsem.at[4]),
+        pltpu.make_async_copy(codes_hbm, codes_ref, wsem.at[5]),
+    ]
+    for copy in input_copies:
+        copy.start()
     barrier = pltpu.get_barrier_semaphore()
-    friends = [z_right, z_left] + [x_dev(d) for d in range(1, NX)]
+    friends = [z_dev(way * d) for d in range(1, STRIDE + 1) for way in (1, -1)]
+    friends += [x_dev(d) for d in range(1, NX)]
     friends += [(node, lax.rem(loc + k, lanes_n)) for k in range(1, lanes_n)]
     for friend in friends:
         pl.semaphore_signal(barrier, inc=1, device_id=friend, device_id_type=MESH)
@@ -112,6 +123,8 @@
     if feats < 256:
         w_down[pl.ds(feats, 256 - feats), :] = jnp.zeros((256 - feats, w_down.shape[1]), BF16)
 
+    for copy in input_copies:
+        copy.wait()
     tokens = tok_ref[...].astype(F32)
     lane4 = iota((TOK, 128), 1)
     ids, codes = ids_ref[...], codes_ref[...].astype(F32)
@@ -120,10 +133,11 @@
     for p in range(ids.shape[1]):
         dense += jnp.where(lane4 == ids[:, p : p + 1], codes[:, p : p + 1], 0.0)
     dense = ROUTE_SCALE * dense / total
-    zb[0, :, pl.ds(0, seg_len)] = jnp.concatenate(
-        [tokens[:, s * seg_len : (s + 1) * seg_len] for s in range(SEG)], axis=0
-    ).astype(BF16)
-    zb[0, :, pl.ds(seg_len, 128)] = jnp.concatenate([dense] * SEG, axis=0).astype(BF16)
+    body = jnp.concatenate([tokens[:, s * seg_len : (s + 1) * seg_len] for s in range(SEG)], axis=0)
+    block = jnp.concatenate([body, jnp.concatenate([dense] * SEG, axis=0)], axis=1).astype(BF16)
+    cut = (seg_len + 128) // PARTS
+    for c in range(PARTS):
+        zb[0, c] = block[:, c * cut : (c + 1) * cut]
 
     pl.semaphore_wait(barrier, len(friends))
     send = Sender(ssem)
@@ -141,36 +155,46 @@
     token_lane = lane_e == ((2 * goal + 2) & 127)
     token_value = ((iota((64, 128), 0) & 3) + 1).astype(F32).astype(BF16)
 
+    x_order = [NX // 2] + [d for d in range(1, NX) if d != NX // 2] + [0]
+
     def select(q):
-        block = zb[pl.ds(4 * q, 4)].reshape(64, seg_len + 128)
+        block = jnp.concatenate([zb[pl.ds(4 * q, 4), c].reshape(64, cut) for c in range(PARTS)], axis=1)
         body, meta = block[:, :seg_len], block[:, seg_len:]
         picks = hot((dot_nt(goal_hot, meta) > 0.0) & same_seg_block)
         rows = dot(picks, body).astype(BF16)
         info = jnp.where(token_lane, dot(picks, token_value), dot(picks, meta)).astype(BF16)
-        for d in list(range(1, NX)) + [0]:
+        for d in x_order:
             target = xs if d else xr
             target[d, q, :, pl.ds(0, seg_len)] = rows[d * 16 : (d + 1) * 16]
             target[d, q, :, pl.ds(seg_len, 128)] = info[d * 16 : (d + 1) * 16]
             if d:
                 send(xs.at[d, q], xr.at[d, q], xsem.at[d, q], x_dev(d))
 
-    def z_hop(j, j_there, device):
-        send(zb.at[at[j]], zb.at[at[j_there]], zsem.at[at[j_there]], device)
-
-    z_hop(0, 1, z_right)
-    z_hop(0, NZ - 1, z_left)
+    reach = {1: NZ // 2, -1: NZ // 2 - 1}
+
+    def z_hop(way, k, step, c):
+        here, there = at[way * k % NZ], at[way * (k + step) % NZ]
+        send(zb.at[here, c], zb.at[there, c], zsem.at[there, c], z_dev(way * step))
+
+    def z_relay(way, k, c):
+        for step in [STRIDE] + list(range(1, STRIDE)):
+            if k % STRIDE == 0 and k + step <= reach[way]:
+                z_hop(way, k, step, c)
+
+    for c in range(PARTS):
+        for way in (1, -1):
+            z_relay(way, 0, c)
     here, done = {0}, 0
-    for k in range(1, NZ // 2 + 1):
-        send.arrived(zb.at[at[k]], zsem.at[at[k]], z_left)
-        here.add(at[k])
-        if k < NZ // 2:
-            z_hop(k, k + 1, z_right)
-        if k < NZ // 2:
-            j = NZ - k
-            send.arrived(zb.at[at[j]], zsem.at[at[j]], z_right)
-            here.add(at[j])
-            if j - 1 > NZ // 2:
-                z_hop(j, j - 1, z_left)
+    for base in range(0, NZ // 2, STRIDE):
+        for k in [base + STRIDE] + list(range(base + 1, base + STRIDE)):
+            for c in range(PARTS):
+                for way in (1, -1):
+                    if k <= reach[way]:
+                        p = at[way * k % NZ]
+                        back = STRIDE if k % STRIDE == 0 else k % STRIDE
+                        send.arrived(zb.at[p, c], zsem.at[p, c], z_dev(-way * back))
+                        z_relay(way, k, c)
+                        here.add(p)
         while done < NZ // 4 and all(p in here for p in range(4 * done, 4 * done + 4)):
             select(done)
             done += 1
@@ -236,11 +260,35 @@
 
     my_expert = lax.div(loc * 128, FF_E)
 
-    def gate_up(chips):
+    pieces = [[0] + ([-1, 1] if half > 1 else [])] + [[-k, k] for k in range(2, half)] + [[half]]
+    starts = [sum(len(p) for p in pieces[:i]) for i in range(len(pieces))]
+    slot = {d % NY: n for n, d in enumerate(d for p in pieces for d in p)}
+    strides = [1 if i < len(pieces) - 2 else 2 for i in range(len(pieces))]
+
+    def h_part(i, lane, k=0, way=0):
+        n = 2 * len(pieces[i])
+        if k < half:
+            return hg.at[lane, pl.ds(2 * starts[i], n)]
+        return hg.at[lane, pl.ds(2 * starts[i] + way * (n // 2), n // 2)]
+
+    def y_dev(d):
+        return (node, chip_lane(d))
+
+    def h_relay(i, way, k, lane):
+        for step in range(strides[i], 0, -1):
+            if k % strides[i] == 0 and k + step <= half:
+                part = h_part(i, lane, k + step, way)
+                send(part, part, hsem.at[i, way, k + step], y_dev(step if way == 0 else -step))
+
+    def hp_hop(i, lane, d, k=0, way=0):
+        sem = hpsem.at[i, NY if k == half and way else d % NY]
+        send(h_part(i, lane, k, way), h_part(i, lane, k, way), sem, partner)
+
+    def gate_up(i):
         lanes = []
-        for d in chips:
+        for d in pieces[i]:
             p_wait(d)
-            lanes += [chip_lane(d), chip_lane(d, True)]
+            lanes += [chip(d) * 2, chip(d) * 2 + 1]
         lhs = jnp.concatenate(
             [jnp.concatenate([xg[lane, s] for lane in lanes], axis=0) for s in range(SEG)], axis=1
         )
@@ -251,8 +299,71 @@
         )
         g, u = pre[:, :128], pre[:, 128:]
         hidden = (gate * (g / (1.0 + jnp.exp(-g))) * u).astype(BF16)
-        for n, lane in enumerate(lanes):
-            hg[loc, lane] = hidden[n * ROWS : (n + 1) * ROWS]
+        for n in range(len(lanes)):
+            hg[loc, 2 * starts[i] + n] = hidden[n * ROWS : (n + 1) * ROWS]
+        hp_hop(i, loc, 0)
+        for way in range(2):
+            h_relay(i, way, 0, loc)
+
+    def h_step(i, k):
+        for way in range(2):
+            d = -k if way == 0 else k
+            lane = chip_lane(d)
+            back = k % strides[i] or strides[i]
+            send.arrived(h_part(i, lane, k, way), hsem.at[i, way, k], y_dev(-back if way == 0 else back))
+            h_relay(i, way, k, lane)
+            hp_hop(i, lane, d, k, way)
+
+    def token_step(k):
+        for h in range(2):
+            for way in range(2):
+                if passes(k, way, h):
+                    d = -k if way == 0 else k
+                    lane = chip_lane(d)
+                    y_wait(way, k, lane, h)
+                    p_hop(d, lane, h, h == way if k < half else way == 0)
+                    if passes(k + 1, way, h):
+                        y_hop(way, k + 1, lane, h)
+
+    group_rows = lanes_n * ROWS
+    back_rows = NZ * lanes_n
+
+    def return_map():
+        info = jnp.concatenate([xm[chip(d) * 2 + c] for d in range(NY) for c in range(2)], axis=0)
+        source = dot_nt(hot(iota((back_rows, 128), 1) == source_at), info)
+        back_r, back_c = iota((back_rows, group_rows), 0), iota((back_rows, group_rows), 1)
+        from_lane = ((y + (back_c >> 5)) & (NY - 1)) * 2 + ((back_c >> 4) & 1)
+        lane_match = (back_r & (lanes_n - 1)) == from_lane
+        back_slot = NZ - 1 - (back_r >> log2(lanes_n))
+        for d in range(NX):
+            ex[d] = hot(lane_match & (source == (back_slot + d * NZ).astype(F32)))
+        token_col[...] = dot(info, hot(iota((128, 128), 0) == token_at))
+
+    def down(d):
+        for i in range(len(pieces)):
+            if not d:
+                send.arrived(h_part(i, chip_lane(d, True)), hpsem.at[i, 0], partner)
+            elif d % NY == half:
+                for way in range(2):
+                    sem = hpsem.at[i, NY if way else d % NY]
+                    send.arrived(h_part(i, chip_lane(d, True), half, way), sem, partner)
+            else:
+                send.arrived(h_part(i, chip_lane(d, True)), hpsem.at[i, d % NY], partner)
+        lhs = jnp.concatenate(
+            [
+                jnp.concatenate(
+                    [
+                        hg[chip(d) * 2 + c, pl.ds(2 * slot[(e - d) % NY], 2)].reshape(2 * ROWS, 128)
+                        for e in range(NY)
+                    ],
+                    axis=0,
+                )
+                for c in range(2)
+            ],
+            axis=1,
+        )
+        at_col = pl.multiple_of(chip(d) * 256, 256)
+        return dot_nt(lhs, w_down[:, pl.ds(at_col, 256)])
 
     for h in range(2):
         for way in range(2):
@@ -261,75 +372,35 @@
         p_hop(0, loc, h, h == 0)
     for copy in weight_copies:
         copy.wait()
-    for k in range(1, half + 1):
-        for h in range(2):
-            for way in range(2):
-                if passes(k, way, h):
-                    d = -k if way == 0 else k
-                    lane = chip_lane(d)
-                    y_wait(way, k, lane, h)
-                    if passes(k + 1, way, h):
-                        y_hop(way, k + 1, lane, h)
-                    p_hop(d, lane, h, h == way if k < half else way == 0)
-        gate_up([0] if k == 1 else [-(k - 1), k - 1])
-    gate_up([half])
-
-    def h_part(lane, h):
-        return hg.at[lane, pl.ds(h * NY, NY)]
-
-    def h_hop(way, k, lane, h):
-        send(h_part(lane, h), h_part(lane, h), hsem.at[way, k, h], y_devs[way])
-
-    def hp_hop(d, lane, h):
-        send(h_part(lane, h), h_part(lane, h), hpsem.at[d % NY, h], partner)
-
-    for h in range(2):
-        for way in range(2):
-            if passes(1, way, h):
-                h_hop(way, 1, loc, h)
-        hp_hop(0, loc, h)
-
-    group_rows = lanes_n * ROWS
-    back_rows = NZ * lanes_n
-    info = xm[...].reshape(group_rows, 128)
-    source = dot_nt(hot(iota((back_rows, 128), 1) == source_at), info)
-    back_r, back_c = iota((back_rows, group_rows), 0), iota((back_rows, group_rows), 1)
-    lane_match = (back_r & (lanes_n - 1)) == (back_c >> 4)
-    back_slot = NZ - 1 - (back_r >> log2(lanes_n))
-    for d in range(NX):
-        ex[d] = hot(lane_match & (source == (back_slot + d * NZ).astype(F32)))
-    token_col = jnp.sum(
-        jnp.where(iota((group_rows, 128), 1) == token_at, info.astype(F32), 0.0), axis=1, keepdims=True
-    )
+
+    def down_step(k):
+        for d in sorted({-k % NY, k}):
+            acc[...] += down(d)
 
     acc[...] = jnp.zeros(acc.shape, F32)
-
-    def down(chips):
-        for d in chips:
-            for h in range(2):
-                send.arrived(h_part(chip_lane(d, True), h), hpsem.at[d % NY, h], partner)
-            lhs = jnp.concatenate(
-                [hg[chip(d) * 2 + c].reshape(group_rows, 128) for c in range(2)], axis=1
-            )
-            at_col = pl.multiple_of(chip(d) * 256, 256)
-            acc[...] += dot_nt(lhs, w_down[:, pl.ds(at_col, 256)])
-
-    for k in range(1, half + 1):
-        for h in range(2):
-            for way in range(2):
-                if passes(k, way, h):
-                    d = -k if way == 0 else k
-                    lane = chip_lane(d)
-                    send.arrived(h_part(lane, h), hsem.at[way, k, h], y_devs[1 - way])
-                    if passes(k + 1, way, h):
-                        h_hop(way, k + 1, lane, h)
-                    hp_hop(d, lane, h)
-        down([0] if k == 1 else [-(k - 1), k - 1])
-    down([half])
-
-    result = jnp.where(iota((group_rows, 256), 1) == feats, token_col, acc[...]).astype(BF16)
+    steps = [(float(k), token_step, (k,)) for k in range(1, half + 1)]
+    for i, piece in enumerate(pieces):
+        far = max(piece)
+        steps.append((min(far + 1, half) + (0.5 if far < half else 0.7), gate_up, (i,)))
+        for k in range(1, half + 1):
+            if strides[i] == 1:
+                when = 0.4 + 0.2 * i if k == 1 else k - 1.0 + 0.1 * i
+            elif i < len(pieces) - 1:
+                when = 1.25 - 0.05 * (k == 2) if k <= 2 else 2.25 + 0.05 * (k == 4)
+            else:
+                when = 1.65 - 0.05 * (k == 2) if k <= 2 else 3.5 + 0.05 * (k == 4)
+            steps.append((half + when, h_step, (i, k)))
+    steps.append((half + 1.4, return_map, ()))
+    for k in range(half + 1):
+        steps.append((half + (3.2 if k < 3 else 4.0), down_step, (k,)))
+    for when, step, operands in sorted(steps, key=lambda entry: entry[0]):
+        step(*operands)
+
+    result = jnp.where(
+        iota((group_rows, 256), 1) == feats, jnp.concatenate([token_col[...]] * 2, axis=1), acc[...]
+    ).astype(BF16)
     for q in range(NZ // 4):
-        for d in list(range(1, NX)) + [0]:
+        for d in x_order:
             rows = dot(ex[d, pl.ds(q * 4 * lanes_n, 4 * lanes_n)], result).astype(BF16)
             target = rs if d else rr
             target[d, pl.ds(4 * q, 4)] = rows.reshape(4, lanes_n, 256)
@@ -355,38 +426,57 @@
                 sums[t] += jnp.where(which == float(t + 1), rows, 0.0)
         return jnp.concatenate(sums, axis=0)
 
-    for s in range(NZ // 2):
-        for j, step, device, source_dev in (
-            (NZ // 2 - s, -1, z_left, z_right),
-            (NZ // 2 + 1 + s, 1, z_right, z_left),
-        ):
-            if j >= NZ:
-                continue
-            value = part(j)
-            if s:
-                send.arrived(rb.at[j], bsem.at[j], source_dev)
-                value += rb[j].astype(F32)
-            sb[j] = value.astype(BF16)
-            send(sb.at[j], rb.at[j + step], bsem.at[j + step], device)
+    def gathered(value, way, k, c):
+        piece = value[:, c * 128 : (c + 1) * 128]
+        slot = at[way * k % NZ] if k else NZ + (way < 0)
+        for step in (1, 2):
+            if k + step <= reach[way]:
+                send.arrived(rb.at[slot, step - 1, c], bsem.at[slot, step - 1, c], z_dev(way * step))
+                piece += rb[slot, step - 1, c].astype(F32)
+        return piece
+
+    def z_send(way, k):
+        step = 1 if k % 2 else 2
+        value = part(way * k % NZ)
+        slot = at[way * k % NZ]
+        there = at[way * (k - step) % NZ] if k > step else NZ + (way < 0)
+        for c in range(2):
+            piece = value[:, c * 128 : (c + 1) * 128] if k % 2 else gathered(value, way, k, c)
+            sb[slot, c] = piece.astype(BF16)
+            send(sb.at[slot, c], rb.at[there, step - 1, c], bsem.at[there, step - 1, c], z_dev(-way * step))
+
+    for k in range(NZ // 2, 0, -2):
+        for way, dist in ((1, k), (-1, k), (-1, k - 1), (1, k - 1)):
+            if k == NZ // 2 and dist <= reach[way]:
+                z_send(way, dist)
+        if k > 2:
+            for way in (1, -1):
+                z_send(way, k - 3)
+            for way in (1, -1):
+                z_send(way, k - 2)
     value = part(0)
-    send.arrived(rb.at[NZ], bsem.at[NZ], z_left)
-    value += rb[NZ].astype(F32)
-    send.arrived(rb.at[0], bsem.at[0], z_right)
-    value = (value + rb[0].astype(F32)).astype(BF16)
+    halves = []
+    for c in range(2):
+        piece = gathered(value, 1, 0, c) + gathered(jnp.zeros(value.shape, F32), -1, 0, c)
+        halves.append(piece.astype(BF16))
 
     fin_r, fin_c = iota((lanes_n * 8, TOK * lanes_n), 0), iota((lanes_n * 8, TOK * lanes_n), 1)
     fin = ((fin_r >> 3) == (fin_c & (lanes_n - 1))) & ((fin_r & 3) == (fin_c >> log2(lanes_n)))
     upper = ((fin_r >> 2) & 1) == 1
-    rows = dot(hot(fin & jnp.logical_not(upper)), value[:, :128]) + dot(hot(fin & upper), value[:, 128:])
+    rows = dot(hot(fin & jnp.logical_not(upper)), halves[0]) + dot(hot(fin & upper), halves[1])
     fs[...] = rows.astype(BF16).reshape(lanes_n, 8, 128)
     for k in range(1, lanes_n):
         lane = lax.rem(loc + k, lanes_n)
         send(fs.at[lane], fr.at[loc], fsem.at[k], (node, lane))
-    out_ref[loc] = fs[loc]
+    fr[loc] = fs[loc]
     for k in range(1, lanes_n):
         lane = lax.rem(loc + lanes_n - k, lanes_n)
         send.arrived(fr.at[lane], fsem.at[k], (node, lane))
-        out_ref[lane] = fr[lane]
+    whole = []
+    for lane in range(lanes_n):
+        piece = fr[lane].astype(F32)
+        whole += [piece[:TOK]] + ([piece[TOK:, : feats - 128]] if feats > 128 else [])
+    out_ref[...] = jnp.concatenate(whole, axis=1).astype(BF16)
     send.drain()
 
 
@@ -399,49 +489,51 @@
     vmem = pl.BlockSpec(memory_space=pltpu.VMEM)
     hbm = pl.BlockSpec(memory_space=pltpu.HBM)
     half = NY // 2
-    pieces = pl.pallas_call(
+    return pl.pallas_call(
         kernel,
-        out_shape=jax.ShapeDtypeStruct((lanes_n, 8, 128), BF16),
-        in_specs=[vmem, vmem, vmem, hbm, hbm, hbm],
+        out_shape=jax.ShapeDtypeStruct((TOK, width), BF16),
+        in_specs=[hbm] * 6,
         out_specs=vmem,
         scratch_shapes=[
+            pltpu.VMEM(tokens.shape, BF16),
+            pltpu.VMEM(expert_ids.shape, I32),
+            pltpu.VMEM(gate_codes.shape, I32),
             pltpu.VMEM((width, 256), BF16),
             pltpu.VMEM((256, hidden), BF16),
-            pltpu.VMEM((NZ, 16, seg_len + 128), BF16),
+            pltpu.VMEM((NZ, PARTS, 16, (seg_len + 128) // PARTS), BF16),
             pltpu.VMEM((NX, NZ // 4, 16, seg_len + 128), BF16),
             pltpu.VMEM((NX, NZ // 4, 16, seg_len + 128), BF16),
             pltpu.VMEM((lanes_n, SEG, ROWS, seg_len), BF16),
             pltpu.VMEM((lanes_n, ROWS, 128), BF16),
             pltpu.VMEM((lanes_n, lanes_n, ROWS, 128), BF16),
             pltpu.VMEM((lanes_n * ROWS, 256), F32),
+            pltpu.VMEM((lanes_n * ROWS, 128), F32),
             pltpu.VMEM((NX, NZ * lanes_n, lanes_n * ROWS), BF16),
             pltpu.VMEM((NX, NZ, lanes_n, 256), BF16),
             pltpu.VMEM((NX, NZ, lanes_n, 256), BF16),
-            pltpu.VMEM((NZ, TOK * lanes_n, 256), BF16),
-            pltpu.VMEM((NZ + 1, TOK * lanes_n, 256), BF16),
+            pltpu.VMEM((NZ, 2, TOK * lanes_n, 128), BF16),
+            pltpu.VMEM((NZ + 2, 2, 2, TOK * lanes_n, 128), BF16),
             pltpu.VMEM((lanes_n, 8, 128), BF16),
             pltpu.VMEM((lanes_n, 8, 128), BF16),
-            dma((3,)),
+            dma((6,)),
             dma((SENDS,)),
-            dma((NZ,)),
+            dma((NZ, PARTS)),
             dma((NX, NZ // 4)),
             dma((2, half + 1, 2)),
             dma((2, half + 1)),
             dma((NY, 2)),
             dma((NY,)),
-            dma((2, half + 1, 2)),
-            dma((NY, 2)),
+            dma((max(half, 2), 2, half + 1)),
+            dma((max(half, 2), NY + 1)),
             dma((NX, NZ // 4)),
-            dma((NZ + 1,)),
+            dma((NZ + 2, 2, 2)),
             dma((lanes_n,)),
         ],
         compiler_params=pltpu.CompilerParams(
-            collective_id=0, has_side_effects=True, vmem_limit_bytes=48 << 20
+            collective_id=0, has_side_effects=True, vmem_limit_bytes=67_000_000
         ),
         name="moe",
     )(tokens, expert_ids, gate_codes, gate_proj, up_proj, down_proj.T)
-    pieces = pieces.reshape(lanes_n, 2, TOK, 128).transpose(2, 0, 1, 3).reshape(TOK, lanes_n, 256)
-    return pieces[:, :, :feats].reshape(TOK, width)
 
 
 def solution(mesh):

time: 124 us -> 102 us (0.82)
  Pallas kernels: 117 us -> 100 us
  local copies, waits for them, and re-layouts: 6.42 us -> 1.37 us
    pallas_call x1, Pallas kernels: 117 us -> 100 us  [on_device(): pl.pallas_call(kernel, out_shape=jax.ShapeDtypeStruct((TOK, width), BF16)...]
    unnamed x12 -> x1, local copies, waits for them, and re-layouts: 5.64 us -> 1.37 us
where the time goes in v2:
time: 102 us; the launch traced here: 101 us
  Pallas kernels  100 us (98%)
  local copies, waits for them, and re-layouts  1.37 us (1%)
    pallas_call x1, Pallas kernels, on_device(): pl.pallas_call(kernel, out_shape=jax.ShapeDtypeStruct((TOK, width), BF16)...  100 us

profile of v2, /device:TPU:1, one launch (start us, length us, event | category | flops | bytes accessed | tf_op | source)
XLA Modules:
  0.0 101.5 jit_solution(11993183845890032233)
XLA Ops:
  0.0 100.1 %moe.1 = bf16[4,3584]{1,0:T(4,128)(2,1)} custom-call(bf16[4,3584]{1,0:T(4,128)(2,1)} %tok_hbm.1, s32[4,6]{1,0:T(4,128)} %ids_hbm.1, s32[4,6]{1,0:T(4,128)} %codes_hbm.1, bf16[3584,128]{1,0:T(8,128)(2,1)} %gate_hbm.1, bf16[3584,128]{1,0:T(8,128)(2,1)} %up_hbm.1, bf16[224,2048]{1,0:T(8,128)(2,1)} %bitcast.1), custom_call_target="tpu_custom_call" | custom-call | tf_op jit(solution)/shard_map/moe/pallas_call | solution.py:492
  100.1 1.4 %copy.8 = bf16[4,3584]{1,0:T(4,128)(2,1)} copy(bf16[4,3584]{1,0:T(4,128)(2,1)} %moe.1) | data formatting | bytes 57344
